TPU v7x, 32 devices: a whole 2x2x4 slice. The times are simulated.
32 devices in a mesh: tm: 16 (over z, x, core), acct: 2 (over y).
Axes of the slice: x: 2, y: 2, z: 4, core: 2. Of those that a mesh axis runs over, the one named last changes fastest.
Arguments:
- returns: bfloat16 [128, 131072], P('tm'), may hold values from -6 to 6
- start: int32 [1], replicated, may hold values from 0 to 131056
- exposures: bfloat16 [512, 131072], P('acct', 'tm'), may hold values from -0.125 to 0.125
- links: int32 [512], replicated, may hold values from 0 to 127
Outputs:
- cov_block: bfloat16 [16, 131072], P('acct', 'tm')
- house_totals: float32 [16, 128], replicated
All inputs are finite; a program needn't handle non-finite values.
Results may differ from a plain program's by a relative error of at most 0.005.
Values may be sent and summed in bfloat16 or wider, within the bound.
A program may use at most 64 MiB of HBM per device.

v0:
```python
import math

import jax
import jax.numpy as jnp
from jax import lax
from jax.sharding import PartitionSpec as P

ROWS_DEV = 8
HOUSES = 128


def day_weights(total_days):
    days = jnp.arange(total_days, dtype=jnp.float32)
    raw = jnp.exp(-math.log(3.0) * (total_days - 1.0 - days) / total_days)
    return raw / jnp.sum(raw)


def on_device(returns, start, exposures, links):
    day_count = returns.shape[0]
    tm_count = lax.axis_size("tm")
    acct_place = lax.axis_index("acct")
    weights = day_weights(day_count * tm_count)
    local_weights = lax.dynamic_slice_in_dim(
        weights, lax.axis_index("tm") * day_count, day_count, 0
    )
    first = start[0] + acct_place * ROWS_DEV
    rows = lax.dynamic_slice_in_dim(returns, first, ROWS_DEV, 1)
    block = (rows.astype(jnp.float32) * local_weights[:, None]).astype(jnp.bfloat16)
    tile_rows = lax.psum_scatter(
        lax.dot_general(
            returns, block, (((0,), (0,)), ((), ())), preferred_element_type=jnp.float32
        ),
        "tm",
        scatter_dimension=0,
        tiled=True,
    )
    cov_tile = tile_rows.T.astype(jnp.bfloat16)
    onehot = (links[:, None] == jnp.arange(HOUSES, dtype=jnp.int32)[None, :]).astype(jnp.float32)
    cov_all = lax.all_gather(cov_tile, "acct", axis=0, tiled=True)
    loads = lax.dot_general(
        cov_all, exposures, (((1,), (1,)), ((), ())), preferred_element_type=jnp.float32
    )
    own_count = exposures.shape[0]
    own_onehot = lax.dynamic_slice_in_dim(onehot, acct_place * own_count, own_count, 0)
    partial_totals = jnp.dot(loads, own_onehot, precision=lax.Precision.HIGHEST)
    house_totals = lax.psum(partial_totals, ("tm", "acct"))
    return (cov_tile, house_totals)


def solution(mesh):
    return jax.shard_map(
        on_device,
        mesh=mesh,
        in_specs=(P("tm", None), P(), P("acct", "tm"), P()),
        out_specs=(P("acct", "tm"), P()),
        check_vma=False,
    )
```

profile of v0, /device:TPU:0, one launch (start us, length us, event | category | flops | bytes accessed | tf_op | source)
XLA Modules:
  0.0 145.9 jit_solution(1166141474180137502)
XLA Ops:
  7.2 0.0 reduce-scatter.2.cloned.1.call-start
  7.2 0.6 fusion.4
  8.5 0.7 broadcast_divide_fusion
  9.2 0.1 dynamic_slice.10
  9.2 4.4 %convolution_bitcast_fusion = f32[131072,8]{0,1:T(8,128)} fusion(bf16[8,131072]{1,0:T(8,128)(2,1)} %param.4, f32[8]{0:T(128)S(1)} %dynamic_slice.10, s32[]{:T(128)S(6)} %select_n.9), kind=kOutput, calls=%fused_computation | convolution fusion | flops 16777408 | bytes 6293540 | tf_op jit(solution)/shard_map/dot_general | solution.py:30
  13.7 0.0 copy-start.1
  13.7 0.0 reduce-scatter.2.cloned.1.call-update
  13.7 0.7 copy-done.1
  14.3 0.1 dynamic-slice
  14.4 74.9 %reduce-scatter.2.cloned.1.call-done = f32[8192,8]{0,1:T(8,128)} async-done(((f32[131072,8]{0,1:T(8,128)}), f32[8192,8]{0,1:T(8,128)}) %reduce-scatter.2.cloned.1.call-update) | async-done | bytes 262160 | tf_op jit(solution)/shard_map/reduce_scatter | solution.py:29
  89.4 1.0 convert_bitcast_fusion
  90.3 0.0 copy-start
  90.3 5.6 %all_gather.3 = bf16[16,8192]{1,0:T(8,128)(2,1)S(1)} all-gather(bf16[8,8192]{1,0:T(8,128)(2,1)S(1)} %convert_bitcast_fusion), channel_id=1, replica_groups=mesh['tm'=16,'acct'=2] {'acct'}, dimensions={0}, use_global_device_ids=true | all-gather | bytes 393216 | tf_op jit(solution)/shard_map/all_gather | solution.py:39
  96.0 3.4 %fusion.6 = f32[16,256]{1,0:T(8,128)S(1)} fusion(bf16[16,8192]{1,0:T(8,128)(2,1)S(1)} %all_gather.3, bf16[256,8192]{1,0:T(8,128)(2,1)} %param.6), kind=kOutput, calls=%fused_computation.12 | convolution fusion | flops 67108864 | bytes 4472832 | tf_op jit(solution)/shard_map/dot_general | solution.py:40
  99.3 0.2 fusion
  99.6 39.5 %psum.7 = f32[16,128]{1,0:T(8,128)} all-reduce(f32[16,128]{1,0:T(8,128)S(1)} %fusion), channel_id=1, replica_groups=mesh['tm'=16,'acct'=2] {'tm','acct'}, use_global_device_ids=true, to_apply=%region_2.0 | all-reduce | flops 2048 | bytes 16384 | tf_op jit(solution)/shard_map/psum | solution.py:46
  139.1 0.0 copy-done
Async XLA Ops:
  7.2 82.2 %reduce-scatter.2.cloned.1.call-start = ((), (), s32[]{:S(2)}) async-start(), calls=%async_computation.1 | async-start | bytes 4456448 | tf_op jit(solution)/shard_map/reduce_scatter | solution.py:29
  13.7 0.7 copy-start.1
  90.3 48.8 %copy-start = (bf16[8,8192]{1,0:T(8,128)(2,1)}, bf16[8,8192]{1,0:T(8,128)(2,1)S(1)}, u32[]{:S(2)}) copy-start(bf16[8,8192]{1,0:T(8,128)(2,1)S(1)} %convert_bitcast_fusion) | copy-start | bytes 393220
Sparse Core Ops, SparseCore 0:
  13.8 75.5 reduce-scatter.1
where the time goes:
time: 146 us
  waiting for transfers between devices  75 us (51%)
  blocking collectives  45.1 us (31%)
  between operations  14.7 us (10%)
  matrix products  8.03 us (5%)
  other arithmetic  2.24 us (2%)
    reduce_scatter x1, waiting for transfers between devices, on_device(): lax.psum_scatter(lax.dot_general(returns, block, (((0,), (0,)), ((), ()))...  74.9 us
    psum x1, blocking collectives, on_device(): house_totals = lax.psum(partial_totals, ('tm', 'acct'))  39.5 us
    all_gather x1, blocking collectives, on_device(): cov_all = lax.all_gather(cov_tile, 'acct', axis=0, tiled=True)  5.64 us
    dot_general x1, matrix products, on_device(): lax.dot_general(returns, block, (((0,), (0,)), ((), ())), preferred_eleme...  4.42 us
    dot_general x1, matrix products, on_device(): lax.dot_general(cov_all, exposures, (((1,), (1,)), ((), ())), preferred_e...  3.37 us
  transfers between devices with their start and end apart: 1, of which 1 were waited for; matrix products, arithmetic and copies ran while one was open for 0% of the time, Pallas kernels for 0%

commit v1 on v0

v1 whole, which is shorter than its diff:
```python
import functools
import math

import jax
import jax.numpy as jnp
from jax import lax
from jax.experimental import pallas as pl
from jax.experimental.pallas import tpu as pltpu
from jax.sharding import PartitionSpec as P

HOUSES = 128
LANES = 128
MESH = pl.DeviceIdType.MESH


def near_root(count):
    return max(d for d in range(1, count + 1) if count % d == 0 and d * d <= count)


def kernel(
    sizes,
    picked_ref, links_ref, returns_hbm, exposures_hbm,
    cov_ref, totals_ref,
    exps, gathered, blocks, turned, slots1, slots2,
    local_sem, dsend, drecv, bsend, brecv, fsend, frecv, send1, recv1, send2, recv2,
):
    tms, accts, low, rows_dev = sizes
    days, factors = returns_hbm.shape
    all_days = days * tms
    rows = rows_dev * accts
    cols = factors // tms
    piece = cols // accts
    own_accounts = exps.shape[0]
    me, acct = lax.axis_index("tm"), lax.axis_index("acct")
    place, layer = lax.rem(me, low), me // low

    def there(shift):
        return lax.rem(me + shift, tms)

    def at_acct(shift):
        return lax.rem(acct + shift, accts)

    own_cols = pl.ds(pl.multiple_of(me * cols, LANES), cols)
    load_own = pltpu.make_async_copy(returns_hbm.at[:, own_cols], gathered.at[me], local_sem.at[0])
    load_own.start()
    load_exps = pltpu.make_async_copy(exposures_hbm, exps, local_sem.at[1])
    load_exps.start()

    barrier = pltpu.get_barrier_semaphore()
    greeted = 0
    for shift in range(1, tms):
        pl.semaphore_signal(barrier, inc=1, device_id=(there(shift), acct), device_id_type=MESH)
        greeted += 1
    for step in range(low):
        for hop in range(1, accts):
            other = layer * low + lax.rem(place + step, low)
            pl.semaphore_signal(barrier, inc=1, device_id=(other, at_acct(hop)), device_id_type=MESH)
            greeted += 1

    def raw_weight(day):
        return jnp.exp(-math.log(3.0) * (all_days - 1.0 - day.astype(jnp.float32)) / all_days)

    total = jnp.sum(
        raw_weight(lax.broadcasted_iota(jnp.int32, (days, all_days), 1)), axis=1, keepdims=True
    )
    weights = raw_weight(me * days + lax.broadcasted_iota(jnp.int32, (days, LANES), 0)) / total
    blocks[me] = (picked_ref[...].astype(jnp.float32) * weights).astype(jnp.bfloat16)

    pl.semaphore_wait(barrier, greeted)

    shifts = sorted(range(1, tms), key=lambda s: -min(s, tms - s))
    own_piece = pl.ds(pl.multiple_of(acct * piece, LANES), piece)
    sends = []
    for shift in shifts:
        copy = pltpu.make_async_remote_copy(
            src_ref=blocks.at[me], dst_ref=blocks.at[me],
            send_sem=bsend.at[shift], recv_sem=brecv.at[shift],
            device_id=(there(shift), acct), device_id_type=MESH,
        )
        copy.start()
        sends.append(copy)
    for shift in shifts:
        to = there(shift)
        out_cols = pl.ds(pl.multiple_of(to * cols + acct * piece, LANES), piece)
        copy = pltpu.make_async_remote_copy(
            src_ref=returns_hbm.at[:, out_cols], dst_ref=gathered.at[me, :, own_piece],
            send_sem=dsend.at[shift], recv_sem=drecv.at[shift],
            device_id=(to, acct), device_id_type=MESH,
        )
        copy.start()
        sends.append(copy)

    def slab(shift, part):
        return gathered.at[there(tms - shift), :, pl.ds(pl.multiple_of(part * piece, LANES), piece)]

    for shift in shifts:
        held = slab(shift, acct)
        pltpu.make_async_remote_copy(
            src_ref=held, dst_ref=held, send_sem=dsend.at[shift], recv_sem=drecv.at[shift],
            device_id=(there(shift), acct), device_id_type=MESH,
        ).wait_recv()
        for hop in range(1, accts):
            copy = pltpu.make_async_remote_copy(
                src_ref=held, dst_ref=held,
                send_sem=fsend.at[hop, shift], recv_sem=frecv.at[hop, shift],
                device_id=(me, at_acct(hop)), device_id_type=MESH,
            )
            copy.start()
            sends.append(copy)

    for shift in shifts:
        block = blocks.at[there(tms - shift)]
        pltpu.make_async_remote_copy(
            src_ref=block, dst_ref=block, send_sem=bsend.at[shift], recv_sem=brecv.at[shift],
            device_id=(there(shift), acct), device_id_type=MESH,
        ).wait_recv()
    turned[...] = blocks[...].astype(jnp.float32).reshape(all_days, LANES).T
    own_rows = turned[pl.ds(pl.multiple_of(acct * rows_dev, rows_dev), rows_dev), :]
    left = jnp.concatenate([turned[:rows, :], own_rows], axis=0).astype(jnp.bfloat16)
    load_own.wait()
    load_exps.wait()

    width = min(piece, 1024)
    loads = jnp.zeros((rows, own_accounts), jnp.float32)
    for turn in range(accts):
        part = at_acct(turn)
        if turn:
            hop = accts - turn
            for shift in shifts:
                held = slab(shift, part)
                pltpu.make_async_remote_copy(
                    src_ref=held, dst_ref=held,
                    send_sem=fsend.at[hop, shift], recv_sem=frecv.at[hop, shift],
                    device_id=(me, at_acct(hop)), device_id_type=MESH,
                ).wait_recv()
        for at in range(0, piece, width):
            span = pl.ds(pl.multiple_of(part * piece + at, LANES), width)
            tile = gathered[:, :, span].astype(jnp.float32).reshape(all_days, width)
            cov = jnp.dot(
                left, tile.astype(jnp.bfloat16), preferred_element_type=jnp.float32
            )
            cov_ref[:, span] = cov[rows:].astype(jnp.bfloat16)
            loads += lax.dot_general(
                cov[:rows].astype(jnp.bfloat16), exps[:, span], (((1,), (1,)), ((), ())),
                preferred_element_type=jnp.float32,
            )

    links = links_ref[:, pl.ds(pl.multiple_of(acct * own_accounts, LANES), own_accounts)]
    house = lax.broadcasted_iota(jnp.int32, (HOUSES, own_accounts), 0)
    member = jnp.where(house == links, 1.0, 0.0)
    mine = place * accts + acct
    slots1[mine] = lax.dot_general(
        loads, member, (((1,), (1,)), ((), ())),
        precision=lax.Precision.HIGHEST, preferred_element_type=jnp.float32,
    )

    group = low * accts
    for step in range(1, group):
        other = layer * low + lax.rem(place + step // accts, low)
        copy = pltpu.make_async_remote_copy(
            src_ref=slots1.at[mine], dst_ref=slots1.at[mine],
            send_sem=send1.at[step], recv_sem=recv1.at[step],
            device_id=(other, at_acct(step % accts)), device_id_type=MESH,
        )
        copy.start()
        sends.append(copy)
    for step in range(1, group):
        sender = lax.rem(place + low - step // accts, low) * accts + at_acct(accts - step % accts)
        pltpu.make_async_remote_copy(
            src_ref=slots1.at[sender], dst_ref=slots1.at[sender],
            send_sem=send1.at[step], recv_sem=recv1.at[step],
            device_id=(me, at_acct(accts - 1)), device_id_type=MESH,
        ).wait_recv()
    slots2[layer] = jnp.sum(slots1[...], axis=0)
    layers = tms // low
    for step in range(1, layers):
        copy = pltpu.make_async_remote_copy(
            src_ref=slots2.at[layer], dst_ref=slots2.at[layer],
            send_sem=send2.at[step], recv_sem=recv2.at[step],
            device_id=(lax.rem(layer + step, layers) * low + place, acct), device_id_type=MESH,
        )
        copy.start()
        sends.append(copy)
    for step in range(1, layers):
        sender = lax.rem(layer + layers - step, layers)
        pltpu.make_async_remote_copy(
            src_ref=slots2.at[sender], dst_ref=slots2.at[sender],
            send_sem=send2.at[step], recv_sem=recv2.at[step],
            device_id=(me, at_acct(accts - 1)), device_id_type=MESH,
        ).wait_recv()
    totals_ref[...] = jnp.sum(slots2[...], axis=0)
    for copy in sends:
        copy.wait_send()


def on_device(tms, accts, returns, start, exposures, links):
    days, factors = returns.shape
    own_accounts, cols = exposures.shape
    rows_dev = 8
    rows = rows_dev * accts
    low = near_root(tms)
    picked = lax.dynamic_slice_in_dim(returns, start[0], rows, 1)
    picked = jnp.pad(picked, ((0, 0), (0, LANES - rows)))
    dma = pltpu.SemaphoreType.DMA
    return pl.pallas_call(
        functools.partial(kernel, (tms, accts, low, rows_dev)),
        out_shape=(
            jax.ShapeDtypeStruct((rows_dev, cols), jnp.bfloat16),
            jax.ShapeDtypeStruct((rows, HOUSES), jnp.float32),
        ),
        in_specs=[
            pl.BlockSpec(memory_space=pltpu.VMEM),
            pl.BlockSpec(memory_space=pltpu.VMEM),
            pl.BlockSpec(memory_space=pl.ANY),
            pl.BlockSpec(memory_space=pl.ANY),
        ],
        out_specs=(
            pl.BlockSpec(memory_space=pltpu.VMEM),
            pl.BlockSpec(memory_space=pltpu.VMEM),
        ),
        scratch_shapes=[
            pltpu.VMEM((own_accounts, cols), exposures.dtype),
            pltpu.VMEM((tms, days, cols), returns.dtype),
            pltpu.VMEM((tms, days, LANES), jnp.bfloat16),
            pltpu.VMEM((LANES, days * tms), jnp.float32),
            pltpu.VMEM((low * accts, rows, HOUSES), jnp.float32),
            pltpu.VMEM((tms // low, rows, HOUSES), jnp.float32),
            dma((2,)),
            dma((tms,)), dma((tms,)), dma((tms,)), dma((tms,)),
            dma((accts, tms)), dma((accts, tms)),
            dma((low * accts,)), dma((low * accts,)),
            dma((tms // low,)), dma((tms // low,)),
        ],
        compiler_params=pltpu.CompilerParams(collective_id=0, has_side_effects=True),
        name="exposures_by_house",
    )(picked, links[None, :], returns, exposures)


def solution(mesh):
    return jax.shard_map(
        functools.partial(on_device, mesh.shape["tm"], mesh.shape["acct"]),
        mesh=mesh,
        in_specs=(P("tm", None), P(), P("acct", "tm"), P()),
        out_specs=(P("acct", "tm"), P()),
        check_vma=False,
    )
```

time: 146 us -> 61.1 us (0.42)
  waiting for transfers between devices: 75 us -> 0 us
  Pallas kernels: 0 us -> 55.3 us
  blocking collectives: 45.1 us -> 0 us
  between operations: 14.7 us -> 1.29 us
  matrix products: 8.03 us -> 0 us
  local copies, waits for them, and re-layouts: 0.81 us -> 4.22 us
  other arithmetic: 2.24 us -> 0 us
    reduce_scatter x1 -> x0, waiting for transfers between devices: 74.9 us -> none  [on_device(): lax.psum_scatter(lax.dot_general(returns, block, (((0,), (0,)), ((), ()))...]
    pallas_call x0 -> x1, Pallas kernels: none -> 55.3 us  [on_device(): pl.pallas_call(functools.partial(kernel, (tms, accts, low, rows_dev)), ou...]
    psum x1 -> x0, blocking collectives: 39.5 us -> none  [on_device(): house_totals = lax.psum(partial_totals, ('tm', 'acct'))]
    dot_general x3 -> x0, matrix products: 8.03 us -> none  [the longest x1 4.42 us: on_device(): lax.dot_general(returns, block, (((0,), (0,)), ((), ())), preferred_eleme...]
    all_gather x1 -> x0, blocking collectives: 5.64 us -> none  [on_device(): cov_all = lax.all_gather(cov_tile, 'acct', axis=0, tiled=True)]
    unnamed x4 -> x2, local copies, waits for them, and re-layouts: 0.66 us -> 2.86 us
  transfers between devices with their start and end apart: 1 -> 0, of which waited for: 1 -> 0; matrix products, arithmetic and copies ran while one was open for 0% -> 0% of each run, Pallas kernels for 0% -> 0%
where the time goes in v1:
time: 61.1 us; the launch traced here: 60.8 us
  Pallas kernels  55.3 us (91%)
  local copies, waits for them, and re-layouts  4.22 us (7%)
  between operations  1.29 us (2%)
    pallas_call x1, Pallas kernels, on_device(): pl.pallas_call(functools.partial(kernel, (tms, accts, low, rows_dev)), ou...  55.3 us
    unnamed x2, local copies, waits for them, and re-layouts  2.86 us

profile of v1, /device:TPU:0, one launch (start us, length us, event | category | flops | bytes accessed | tf_op | source)
XLA Modules:
  0.0 60.8 jit_solution(4140575220901711764)
XLA Ops:
  1.3 0.8 %constant_dynamic-slice_fusion = bf16[8,16]{1,0:T(8,128)(2,1)S(1)} fusion(bf16[8,131072]{1,0:T(8,128)(2,1)} %returns_hbm.1, s32[]{:T(128)S(6)} %select_n.3), kind=kLoop, calls=%fused_computation | loop fusion | bytes 516 | tf_op jit(solution)/shard_map/dynamic_slice | solution.py:202
  2.0 0.6 pad.4.picked_ref
  2.6 55.3 %exposures_by_house.1 = (bf16[8,8192]{1,0:T(8,128)(2,1)}, f32[16,128]{1,0:T(8,128)}) custom-call(bf16[8,128]{1,0:T(8,128)(2,1)} %pad.4.picked_ref, s32[1,512]{1,0:T(1,128)} %bitcast.5, bf16[8,131072]{1,0:T(8,128)(2,1)} %returns_hbm.1, bf16[256,8192]{1,0:T(8,128)(2,1)} %exposures_hbm.1), custom_call_target="tpu_custom_call" | custom-call | tf_op jit(solution)/shard_map/exposures_by_house/pallas_call | solution.py:205
  57.9 1.6 %copy.9 = bf16[8,8192]{1,0:T(8,128)(2,1)} copy(bf16[8,8192]{1,0:T(8,128)(2,1)} %get-tuple-element.4) | data formatting | bytes 262144
  59.5 1.3 %copy.10 = f32[16,128]{1,0:T(8,128)} copy(f32[16,128]{1,0:T(8,128)} %get-tuple-element.5) | data formatting | bytes 16384

commit v2 on v1

--- a/solution.py
+++ b/solution.py
@@ -19,9 +19,9 @@
 
 def kernel(
     sizes,
-    picked_ref, links_ref, returns_hbm, exposures_hbm,
-    cov_ref, totals_ref,
-    exps, gathered, blocks, turned, slots1, slots2,
+    start_ref, window_ref, links_ref, returns_hbm, exposures_hbm,
+    cov_hbm, totals_ref,
+    exps, gathered, blocks, turned, covs, slots1, slots2,
     local_sem, dsend, drecv, bsend, brecv, fsend, frecv, send1, recv1, send2, recv2,
 ):
     tms, accts, low, rows_dev = sizes
@@ -40,7 +40,7 @@
     def at_acct(shift):
         return lax.rem(acct + shift, accts)
 
-    own_cols = pl.ds(pl.multiple_of(me * cols, LANES), cols)
+    own_cols = pl.ds(pl.multiple_of(me * cols + acct * piece, LANES), piece)
     load_own = pltpu.make_async_copy(returns_hbm.at[:, own_cols], gathered.at[me], local_sem.at[0])
     load_own.start()
     load_exps = pltpu.make_async_copy(exposures_hbm, exps, local_sem.at[1])
@@ -57,6 +57,13 @@
             pl.semaphore_signal(barrier, inc=1, device_id=(other, at_acct(hop)), device_id_type=MESH)
             greeted += 1
 
+    offset = start_ref[0] - jnp.minimum(start_ref[0], factors - LANES)
+    source = lax.broadcasted_iota(jnp.int32, (LANES, LANES), 0)
+    target = lax.broadcasted_iota(jnp.int32, (LANES, LANES), 1)
+    pick = jnp.where((source == target + offset) & (target < rows), 1.0, 0.0)
+    picked = jnp.dot(
+        window_ref[...], pick.astype(jnp.bfloat16), preferred_element_type=jnp.float32
+    )
     def raw_weight(day):
         return jnp.exp(-math.log(3.0) * (all_days - 1.0 - day.astype(jnp.float32)) / all_days)
 
@@ -64,12 +71,11 @@
         raw_weight(lax.broadcasted_iota(jnp.int32, (days, all_days), 1)), axis=1, keepdims=True
     )
     weights = raw_weight(me * days + lax.broadcasted_iota(jnp.int32, (days, LANES), 0)) / total
-    blocks[me] = (picked_ref[...].astype(jnp.float32) * weights).astype(jnp.bfloat16)
+    blocks[me] = (picked * weights).astype(jnp.bfloat16)
 
     pl.semaphore_wait(barrier, greeted)
 
     shifts = sorted(range(1, tms), key=lambda s: -min(s, tms - s))
-    own_piece = pl.ds(pl.multiple_of(acct * piece, LANES), piece)
     sends = []
     for shift in shifts:
         copy = pltpu.make_async_remote_copy(
@@ -79,32 +85,24 @@
         )
         copy.start()
         sends.append(copy)
-    for shift in shifts:
+    last = max(LANES, piece // 4 // LANES * LANES)
+    parts = [(at, size) for at, size in ((0, piece - last), (piece - last, last)) if size]
+
+    def direct(index, shift, slot):
+        at, size = parts[index]
         to = there(shift)
-        out_cols = pl.ds(pl.multiple_of(to * cols + acct * piece, LANES), piece)
-        copy = pltpu.make_async_remote_copy(
-            src_ref=returns_hbm.at[:, out_cols], dst_ref=gathered.at[me, :, own_piece],
-            send_sem=dsend.at[shift], recv_sem=drecv.at[shift],
+        return pltpu.make_async_remote_copy(
+            src_ref=returns_hbm.at[
+                :, pl.ds(pl.multiple_of(to * cols + acct * piece + at, LANES), size)
+            ],
+            dst_ref=gathered.at[slot, :, pl.ds(at, size)],
+            send_sem=dsend.at[index, shift], recv_sem=drecv.at[index, shift],
             device_id=(to, acct), device_id_type=MESH,
         )
-        copy.start()
-        sends.append(copy)
-
-    def slab(shift, part):
-        return gathered.at[there(tms - shift), :, pl.ds(pl.multiple_of(part * piece, LANES), piece)]
-
-    for shift in shifts:
-        held = slab(shift, acct)
-        pltpu.make_async_remote_copy(
-            src_ref=held, dst_ref=held, send_sem=dsend.at[shift], recv_sem=drecv.at[shift],
-            device_id=(there(shift), acct), device_id_type=MESH,
-        ).wait_recv()
-        for hop in range(1, accts):
-            copy = pltpu.make_async_remote_copy(
-                src_ref=held, dst_ref=held,
-                send_sem=fsend.at[hop, shift], recv_sem=frecv.at[hop, shift],
-                device_id=(me, at_acct(hop)), device_id_type=MESH,
-            )
+
+    for index in range(len(parts)):
+        for shift in shifts:
+            copy = direct(index, shift, me)
             copy.start()
             sends.append(copy)
 
@@ -115,35 +113,54 @@
             device_id=(there(shift), acct), device_id_type=MESH,
         ).wait_recv()
     turned[...] = blocks[...].astype(jnp.float32).reshape(all_days, LANES).T
-    own_rows = turned[pl.ds(pl.multiple_of(acct * rows_dev, rows_dev), rows_dev), :]
-    left = jnp.concatenate([turned[:rows, :], own_rows], axis=0).astype(jnp.bfloat16)
+    left = turned[:rows, :].astype(jnp.bfloat16)
     load_own.wait()
     load_exps.wait()
 
-    width = min(piece, 1024)
+    def columns(owner, at, size):
+        return pl.ds(pl.multiple_of(owner * piece + at, LANES), size)
+
+    def exchange(index, hop, owner):
+        held = covs.at[:, :, columns(owner, *parts[index])]
+        return pltpu.make_async_remote_copy(
+            src_ref=held, dst_ref=held,
+            send_sem=fsend.at[index, hop], recv_sem=frecv.at[index, hop],
+            device_id=(me, at_acct(hop)), device_id_type=MESH,
+        )
+
+    def loads_of(owner, index):
+        span = columns(owner, *parts[index])
+        cov = covs[:, :, span].astype(jnp.float32).reshape(rows, parts[index][1])
+        return lax.dot_general(
+            cov.astype(jnp.bfloat16), exps[:, span], (((1,), (1,)), ((), ())),
+            preferred_element_type=jnp.float32,
+        )
+
     loads = jnp.zeros((rows, own_accounts), jnp.float32)
-    for turn in range(accts):
-        part = at_acct(turn)
-        if turn:
-            hop = accts - turn
-            for shift in shifts:
-                held = slab(shift, part)
-                pltpu.make_async_remote_copy(
-                    src_ref=held, dst_ref=held,
-                    send_sem=fsend.at[hop, shift], recv_sem=frecv.at[hop, shift],
-                    device_id=(me, at_acct(hop)), device_id_type=MESH,
-                ).wait_recv()
-        for at in range(0, piece, width):
-            span = pl.ds(pl.multiple_of(part * piece + at, LANES), width)
-            tile = gathered[:, :, span].astype(jnp.float32).reshape(all_days, width)
+    for index, (first, size) in enumerate(parts):
+        for shift in shifts:
+            direct(index, shift, there(tms - shift)).wait_recv()
+        width = math.gcd(size, 1024)
+        for at in range(first, first + size, width):
+            tile = gathered[:, :, pl.ds(at, width)].astype(jnp.float32)
             cov = jnp.dot(
-                left, tile.astype(jnp.bfloat16), preferred_element_type=jnp.float32
-            )
-            cov_ref[:, span] = cov[rows:].astype(jnp.bfloat16)
-            loads += lax.dot_general(
-                cov[:rows].astype(jnp.bfloat16), exps[:, span], (((1,), (1,)), ((), ())),
+                left, tile.reshape(all_days, width).astype(jnp.bfloat16),
                 preferred_element_type=jnp.float32,
             )
+            covs[:, :, columns(acct, at, width)] = cov.reshape(accts, rows_dev, width).astype(
+                jnp.bfloat16
+            )
+        for hop in range(1, accts):
+            copy = exchange(index, hop, acct)
+            copy.start()
+            sends.append(copy)
+        loads += loads_of(acct, index)
+        for hop in range(1, accts):
+            owner = at_acct(accts - hop)
+            exchange(index, hop, owner).wait_recv()
+            loads += loads_of(owner, index)
+    store_cov = pltpu.make_async_copy(covs.at[acct], cov_hbm, local_sem.at[0])
+    store_cov.start()
 
     links = links_ref[:, pl.ds(pl.multiple_of(acct * own_accounts, LANES), own_accounts)]
     house = lax.broadcasted_iota(jnp.int32, (HOUSES, own_accounts), 0)
@@ -191,6 +208,7 @@
     totals_ref[...] = jnp.sum(slots2[...], axis=0)
     for copy in sends:
         copy.wait_send()
+    store_cov.wait()
 
 
 def on_device(tms, accts, returns, start, exposures, links):
@@ -199,8 +217,9 @@
     rows_dev = 8
     rows = rows_dev * accts
     low = near_root(tms)
-    picked = lax.dynamic_slice_in_dim(returns, start[0], rows, 1)
-    picked = jnp.pad(picked, ((0, 0), (0, LANES - rows)))
+    window = lax.dynamic_slice_in_dim(
+        returns, jnp.minimum(start[0], factors - LANES), LANES, 1
+    )
     dma = pltpu.SemaphoreType.DMA
     return pl.pallas_call(
         functools.partial(kernel, (tms, accts, low, rows_dev)),
@@ -209,31 +228,33 @@
             jax.ShapeDtypeStruct((rows, HOUSES), jnp.float32),
         ),
         in_specs=[
+            pl.BlockSpec(memory_space=pltpu.SMEM),
             pl.BlockSpec(memory_space=pltpu.VMEM),
             pl.BlockSpec(memory_space=pltpu.VMEM),
             pl.BlockSpec(memory_space=pl.ANY),
             pl.BlockSpec(memory_space=pl.ANY),
         ],
         out_specs=(
-            pl.BlockSpec(memory_space=pltpu.VMEM),
+            pl.BlockSpec(memory_space=pl.ANY),
             pl.BlockSpec(memory_space=pltpu.VMEM),
         ),
         scratch_shapes=[
             pltpu.VMEM((own_accounts, cols), exposures.dtype),
-            pltpu.VMEM((tms, days, cols), returns.dtype),
+            pltpu.VMEM((tms, days, cols // accts), returns.dtype),
             pltpu.VMEM((tms, days, LANES), jnp.bfloat16),
             pltpu.VMEM((LANES, days * tms), jnp.float32),
+            pltpu.VMEM((accts, rows_dev, cols), jnp.bfloat16),
             pltpu.VMEM((low * accts, rows, HOUSES), jnp.float32),
             pltpu.VMEM((tms // low, rows, HOUSES), jnp.float32),
             dma((2,)),
-            dma((tms,)), dma((tms,)), dma((tms,)), dma((tms,)),
-            dma((accts, tms)), dma((accts, tms)),
+            dma((2, tms)), dma((2, tms)), dma((tms,)), dma((tms,)),
+            dma((2, accts)), dma((2, accts)),
             dma((low * accts,)), dma((low * accts,)),
             dma((tms // low,)), dma((tms // low,)),
         ],
         compiler_params=pltpu.CompilerParams(collective_id=0, has_side_effects=True),
         name="exposures_by_house",
-    )(picked, links[None, :], returns, exposures)
+    )(start, window, links[None, :], returns, exposures)
 
 
 def solution(mesh):

time: 61.1 us -> 52 us (0.85)
  Pallas kernels: 55.3 us -> 46.2 us
    pallas_call x1, Pallas kernels: 55.3 us -> 46.2 us  [on_device(): pl.pallas_call(functools.partial(kernel, (tms, accts, low, rows_dev)), ou...]
where the time goes in v2:
time: 52 us; the launch traced here: 51.7 us
  Pallas kernels  46.2 us (89%)
  local copies, waits for them, and re-layouts  4.21 us (8%)
  between operations  1.29 us (2%)
    pallas_call x1, Pallas kernels, on_device(): pl.pallas_call(functools.partial(kernel, (tms, accts, low, rows_dev)), ou...  46.2 us
    unnamed x2, local copies, waits for them, and re-layouts  2.86 us
    dynamic_slice x1, local copies, waits for them, and re-layouts, on_device(): lax.dynamic_slice_in_dim(returns, jnp.minimum(start[0], factors - LANES),...  1.34 us

profile of v2, /device:TPU:0, one launch (start us, length us, event | category | flops | bytes accessed | tf_op | source)
XLA Modules:
  0.0 51.7 jit_solution(10004993575144387355)
XLA Ops:
  1.3 1.3 %constant_dynamic-slice_fusion.window_ref = bf16[8,128]{1,0:T(8,128)(2,1)} fusion(bf16[8,131072]{1,0:T(8,128)(2,1)} %returns_hbm.1, s32[]{:T(128)S(6)} %select_n.3), kind=kLoop, calls=%fused_computation | loop fusion | bytes 4100 | tf_op jit(solution)/shard_map/dynamic_slice | solution.py:220
  2.6 46.2 %exposures_by_house.1 = (bf16[8,8192]{1,0:T(8,128)(2,1)}, f32[16,128]{1,0:T(8,128)}) custom-call(s32[1]{0:T(128)S(6)} %copy.8.start_ref, bf16[8,128]{1,0:T(8,128)(2,1)} %constant_dynamic-slice_fusion.window_ref, s32[1,512]{1,0:T(1,128)} %bitcast.2, bf16[8,131072]{1,0:T(8,128)(2,1)} %returns_hbm.1, bf16[256,8192]{1,0:T(8,128)(2,1)} %exposures_hbm.1), custom_call_target="tpu_custom_call" | custom-call | tf_op jit(solution)/shard_map/exposures_by_house/pallas_call | solution.py:224
  48.8 1.6 %copy.9 = bf16[8,8192]{1,0:T(8,128)(2,1)} copy(bf16[8,8192]{1,0:T(8,128)(2,1)} %get-tuple-element.4) | data formatting | bytes 262144
  50.4 1.3 %copy.10 = f32[16,128]{1,0:T(8,128)} copy(f32[16,128]{1,0:T(8,128)} %get-tuple-element.5) | data formatting | bytes 16384

commit v3 on v2

--- a/solution.py
+++ b/solution.py
@@ -19,9 +19,9 @@
 
 def kernel(
     sizes,
-    start_ref, window_ref, links_ref, returns_hbm, exposures_hbm,
+    start_ref, links_ref, tiles_hbm, returns_hbm, exposures_hbm,
     cov_hbm, totals_ref,
-    exps, gathered, blocks, turned, covs, slots1, slots2,
+    tiles, exps, gathered, blocks, turned, covs, slots1, slots2,
     local_sem, dsend, drecv, bsend, brecv, fsend, frecv, send1, recv1, send2, recv2,
 ):
     tms, accts, low, rows_dev = sizes
@@ -41,6 +41,8 @@
         return lax.rem(acct + shift, accts)
 
     own_cols = pl.ds(pl.multiple_of(me * cols + acct * piece, LANES), piece)
+    load_tiles = pltpu.make_async_copy(tiles_hbm, tiles, local_sem.at[2])
+    load_tiles.start()
     load_own = pltpu.make_async_copy(returns_hbm.at[:, own_cols], gathered.at[me], local_sem.at[0])
     load_own.start()
     load_exps = pltpu.make_async_copy(exposures_hbm, exps, local_sem.at[1])
@@ -57,13 +59,18 @@
             pl.semaphore_signal(barrier, inc=1, device_id=(other, at_acct(hop)), device_id_type=MESH)
             greeted += 1
 
-    offset = start_ref[0] - jnp.minimum(start_ref[0], factors - LANES)
-    source = lax.broadcasted_iota(jnp.int32, (LANES, LANES), 0)
-    target = lax.broadcasted_iota(jnp.int32, (LANES, LANES), 1)
+    load_tiles.wait()
+    tile_count = tiles.shape[0]
+    first_tile = lax.div(start_ref[0], LANES)
+    window = jnp.concatenate(
+        [tiles[first_tile], tiles[jnp.minimum(first_tile + 1, tile_count - 1)]], axis=1
+    )
+    offset = start_ref[0] - first_tile * LANES
+    source = lax.broadcasted_iota(jnp.int32, (2 * LANES, LANES), 0)
+    target = lax.broadcasted_iota(jnp.int32, (2 * LANES, LANES), 1)
     pick = jnp.where((source == target + offset) & (target < rows), 1.0, 0.0)
-    picked = jnp.dot(
-        window_ref[...], pick.astype(jnp.bfloat16), preferred_element_type=jnp.float32
-    )
+    picked = jnp.dot(window, pick.astype(jnp.bfloat16), preferred_element_type=jnp.float32)
+
     def raw_weight(day):
         return jnp.exp(-math.log(3.0) * (all_days - 1.0 - day.astype(jnp.float32)) / all_days)
 
@@ -211,17 +218,20 @@
     store_cov.wait()
 
 
+def hand_over(cov_ref, totals_ref, cov_out, totals_out):
+    cov_out[...] = cov_ref[...]
+    totals_out[...] = totals_ref[...]
+
+
 def on_device(tms, accts, returns, start, exposures, links):
     days, factors = returns.shape
     own_accounts, cols = exposures.shape
     rows_dev = 8
     rows = rows_dev * accts
     low = near_root(tms)
-    window = lax.dynamic_slice_in_dim(
-        returns, jnp.minimum(start[0], factors - LANES), LANES, 1
-    )
+    tiles = returns.reshape(days, factors // LANES, LANES).transpose(1, 0, 2)
     dma = pltpu.SemaphoreType.DMA
-    return pl.pallas_call(
+    cov, totals = pl.pallas_call(
         functools.partial(kernel, (tms, accts, low, rows_dev)),
         out_shape=(
             jax.ShapeDtypeStruct((rows_dev, cols), jnp.bfloat16),
@@ -230,7 +240,7 @@
         in_specs=[
             pl.BlockSpec(memory_space=pltpu.SMEM),
             pl.BlockSpec(memory_space=pltpu.VMEM),
-            pl.BlockSpec(memory_space=pltpu.VMEM),
+            pl.BlockSpec(memory_space=pl.ANY),
             pl.BlockSpec(memory_space=pl.ANY),
             pl.BlockSpec(memory_space=pl.ANY),
         ],
@@ -239,6 +249,7 @@
             pl.BlockSpec(memory_space=pltpu.VMEM),
         ),
         scratch_shapes=[
+            pltpu.VMEM((factors // LANES, days, LANES), returns.dtype),
             pltpu.VMEM((own_accounts, cols), exposures.dtype),
             pltpu.VMEM((tms, days, cols // accts), returns.dtype),
             pltpu.VMEM((tms, days, LANES), jnp.bfloat16),
@@ -246,7 +257,7 @@
             pltpu.VMEM((accts, rows_dev, cols), jnp.bfloat16),
             pltpu.VMEM((low * accts, rows, HOUSES), jnp.float32),
             pltpu.VMEM((tms // low, rows, HOUSES), jnp.float32),
-            dma((2,)),
+            dma((3,)),
             dma((2, tms)), dma((2, tms)), dma((tms,)), dma((tms,)),
             dma((2, accts)), dma((2, accts)),
             dma((low * accts,)), dma((low * accts,)),
@@ -254,7 +265,17 @@
         ],
         compiler_params=pltpu.CompilerParams(collective_id=0, has_side_effects=True),
         name="exposures_by_house",
-    )(start, window, links[None, :], returns, exposures)
+    )(start, links[None, :], tiles, returns, exposures)
+    return pl.pallas_call(
+        hand_over,
+        out_shape=(
+            jax.ShapeDtypeStruct(cov.shape, cov.dtype),
+            jax.ShapeDtypeStruct(totals.shape, totals.dtype),
+        ),
+        in_specs=[pl.BlockSpec(memory_space=pltpu.VMEM)] * 2,
+        out_specs=(pl.BlockSpec(memory_space=pltpu.VMEM),) * 2,
+        name="hand_over",
+    )(cov, totals)
 
 
 def solution(mesh):

time: 52 us -> 49.2 us (0.946)
  local copies, waits for them, and re-layouts: 4.21 us -> 0 us
  Pallas kernels: 46.2 us -> 47.8 us
    unnamed x2 -> x0, local copies, waits for them, and re-layouts: 2.86 us -> none
    pallas_call x0 -> x1, Pallas kernels: none -> 1.57 us  [on_device(): pl.pallas_call(hand_over, out_shape=(jax.ShapeDtypeStruct(cov.shape, cov....]
    dynamic_slice x1 -> x0, local copies, waits for them, and re-layouts: 1.34 us -> none  [on_device(): lax.dynamic_slice_in_dim(returns, jnp.minimum(start[0], factors - LANES),...]
where the time goes in v3:
time: 49.2 us; the launch traced here: 49 us
  Pallas kernels  47.8 us (97%)
  between operations  1.28 us (3%)
    pallas_call x1, Pallas kernels, on_device(): pl.pallas_call(functools.partial(kernel, (tms, accts, low, rows_dev)), ou...  46.2 us
    pallas_call x1, Pallas kernels, on_device(): pl.pallas_call(hand_over, out_shape=(jax.ShapeDtypeStruct(cov.shape, cov....  1.57 us

profile of v3, /device:TPU:0, one launch (start us, length us, event | category | flops | bytes accessed | tf_op | source)
XLA Modules:
  0.0 49.0 jit_solution(7628760790624352242)
XLA Ops:
  1.3 46.2 %exposures_by_house.1 = (bf16[8,8192]{1,0:T(8,128)(2,1)}, f32[16,128]{1,0:T(8,128)}) custom-call(s32[1]{0:T(128)S(6)} %copy.6.start_ref, s32[1,512]{1,0:T(1,128)} %bitcast.5, bf16[1024,8,128]{2,1,0:T(8,128)(2,1)} %bitcast.4, bf16[8,131072]{1,0:T(8,128)(2,1)} %returns_hbm.1, bf16[256,8192]{1,0:T(8,128)(2,1)} %exposures_hbm.1), custom_call_target="tpu_custom_call" | custom-call | tf_op jit(solution)/shard_map/exposures_by_house/pallas_call | solution.py:234
  47.5 1.6 %hand_over.1 = (bf16[8,8192]{1,0:T(8,128)(2,1)}, f32[16,128]{1,0:T(8,128)}) custom-call(bf16[8,8192]{1,0:T(8,128)(2,1)} %get-tuple-element.4.cov_ref, f32[16,128]{1,0:T(8,128)} %get-tuple-element.5.totals_ref), custom_call_target="tpu_custom_call" | custom-call | tf_op jit(solution)/shard_map/hand_over/pallas_call | solution.py:269

commit v4 on v3

--- a/solution.py
+++ b/solution.py
@@ -82,7 +82,7 @@
 
     pl.semaphore_wait(barrier, greeted)
 
-    shifts = sorted(range(1, tms), key=lambda s: -min(s, tms - s))
+    shifts = [*range(tms // 2, tms), *range(tms // 2 - 1, 0, -1)]
     sends = []
     for shift in shifts:
         copy = pltpu.make_async_remote_copy(
@@ -92,7 +92,7 @@
         )
         copy.start()
         sends.append(copy)
-    last = max(LANES, piece // 4 // LANES * LANES)
+    last = max(LANES, piece // 2 // LANES * LANES)
     parts = [(at, size) for at, size in ((0, piece - last), (piece - last, last)) if size]
 
     def direct(index, shift, slot):

time: 49.2 us -> 46.8 us (0.951)
  Pallas kernels: 47.8 us -> 45.3 us
    pallas_call x1, Pallas kernels: 46.2 us -> 43.7 us  [on_device(): pl.pallas_call(functools.partial(kernel, (tms, accts, low, rows_dev)), ou...]
where the time goes in v4:
time: 46.8 us; the launch traced here: 46.6 us
  Pallas kernels  45.3 us (97%)
  between operations  1.28 us (3%)
    pallas_call x1, Pallas kernels, on_device(): pl.pallas_call(functools.partial(kernel, (tms, accts, low, rows_dev)), ou...  43.7 us
    pallas_call x1, Pallas kernels, on_device(): pl.pallas_call(hand_over, out_shape=(jax.ShapeDtypeStruct(cov.shape, cov....  1.57 us

profile of v4, /device:TPU:0, one launch (start us, length us, event | category | flops | bytes accessed | tf_op | source)
XLA Modules:
  0.0 46.6 jit_solution(17559440283120534827)
XLA Ops:
  1.3 43.7 %exposures_by_house.1 = (bf16[8,8192]{1,0:T(8,128)(2,1)}, f32[16,128]{1,0:T(8,128)}) custom-call(s32[1]{0:T(128)S(6)} %copy.6.start_ref, s32[1,512]{1,0:T(1,128)} %bitcast.5, bf16[1024,8,128]{2,1,0:T(8,128)(2,1)} %bitcast.4, bf16[8,131072]{1,0:T(8,128)(2,1)} %returns_hbm.1, bf16[256,8192]{1,0:T(8,128)(2,1)} %exposures_hbm.1), custom_call_target="tpu_custom_call" | custom-call | tf_op jit(solution)/shard_map/exposures_by_house/pallas_call | solution.py:234
  45.0 1.6 %hand_over.1 = (bf16[8,8192]{1,0:T(8,128)(2,1)}, f32[16,128]{1,0:T(8,128)}) custom-call(bf16[8,8192]{1,0:T(8,128)(2,1)} %get-tuple-element.4.cov_ref, f32[16,128]{1,0:T(8,128)} %get-tuple-element.5.totals_ref), custom_call_target="tpu_custom_call" | custom-call | tf_op jit(solution)/shard_map/hand_over/pallas_call | solution.py:269

commit v5 on v4

--- a/solution.py
+++ b/solution.py
@@ -13,8 +13,8 @@
 MESH = pl.DeviceIdType.MESH
 
 
-def near_root(count):
-    return max(d for d in range(1, count + 1) if count % d == 0 and d * d <= count)
+def least_divisor(count):
+    return min((d for d in range(2, count + 1) if count % d == 0), default=1)
 
 
 def kernel(
@@ -228,7 +228,7 @@
     own_accounts, cols = exposures.shape
     rows_dev = 8
     rows = rows_dev * accts
-    low = near_root(tms)
+    low = least_divisor(tms)
     tiles = returns.reshape(days, factors // LANES, LANES).transpose(1, 0, 2)
     dma = pltpu.SemaphoreType.DMA
     cov, totals = pl.pallas_call(

time: 46.8 us -> 46.7 us (level)
  no operation moved by 1% of the time
where the time goes in v5:
time: 46.7 us; the launch traced here: 46.5 us
  Pallas kernels  45.2 us (97%)
  between operations  1.28 us (3%)
    pallas_call x1, Pallas kernels, on_device(): pl.pallas_call(functools.partial(kernel, (tms, accts, low, rows_dev)), ou...  43.6 us
    pallas_call x1, Pallas kernels, on_device(): pl.pallas_call(hand_over, out_shape=(jax.ShapeDtypeStruct(cov.shape, cov....  1.57 us

profile of v5, /device:TPU:0, one launch (start us, length us, event | category | flops | bytes accessed | tf_op | source)
XLA Modules:
  0.0 46.5 jit_solution(9462521384396807808)
XLA Ops:
  1.3 43.6 %exposures_by_house.1 = (bf16[8,8192]{1,0:T(8,128)(2,1)}, f32[16,128]{1,0:T(8,128)}) custom-call(s32[1]{0:T(128)S(6)} %copy.6.start_ref, s32[1,512]{1,0:T(1,128)} %bitcast.5, bf16[1024,8,128]{2,1,0:T(8,128)(2,1)} %bitcast.4, bf16[8,131072]{1,0:T(8,128)(2,1)} %returns_hbm.1, bf16[256,8192]{1,0:T(8,128)(2,1)} %exposures_hbm.1), custom_call_target="tpu_custom_call" | custom-call | tf_op jit(solution)/shard_map/exposures_by_house/pallas_call | solution.py:234
  44.9 1.6 %hand_over.1 = (bf16[8,8192]{1,0:T(8,128)(2,1)}, f32[16,128]{1,0:T(8,128)}) custom-call(bf16[8,8192]{1,0:T(8,128)(2,1)} %get-tuple-element.4.cov_ref, f32[16,128]{1,0:T(8,128)} %get-tuple-element.5.totals_ref), custom_call_target="tpu_custom_call" | custom-call | tf_op jit(solution)/shard_map/hand_over/pallas_call | solution.py:269
